TPU v7x, 256 devices: a whole 4x4x8 slice. The times are simulated.
256 devices in a mesh: gen: 8 (over z_lo, core), user: 16 (over x, y), cand: 2 (over z_hi).
Axes of the slice: x: 4, y: 4, z: 8 (z_hi: 2, z_lo: 4; z = z_hi * 4 + z_lo), core: 2. Of those that a mesh axis runs over, the one named last changes fastest.
Arguments:
- states: bfloat16 [16384, 4096], P(('user', 'cand')), may hold values from -6 to 6
- norm_gain: float32 [4096], replicated, may hold values from 0.1 to 1.9
- gate_weight: bfloat16 [4096, 7168], P('user', 'gen'), may hold values from -0.09375 to 0.09375
- up_weight: bfloat16 [4096, 7168], P('user', 'gen'), may hold values from -0.09375 to 0.09375
- down_weight: bfloat16 [7168, 4096], P('gen', 'user'), may hold values from -0.0625 to 0.0625
- proj_weight: bfloat16 [4096, 1024], P('gen'), may hold values from -0.09375 to 0.09375
- private_rows: bfloat16 [32768, 1024], P(('gen', 'user')), may hold values from -6 to 6
- enc_weight: bfloat16 [1024, 1024], replicated, may hold values from -0.1875 to 0.1875
- user_ids: int32 [32768], P(('gen', 'user')), may hold values from 0 to 31
Outputs:
- votes: float32 [16, 2, 128], P(None, 'cand')
Inputs may be any that keep to these rules, and one draw needn't show every extreme that they name: `user_ids`: a user is a pair of a block of 256 rows and a slot; no user has rows in two blocks.
All inputs are finite; a program needn't handle non-finite values.
Results may differ from a plain program's by a relative error of at most 0.0025.
Values may be sent and summed in bfloat16 or wider, within the bound.
No kernel may reach another device: no remote copies, remote signals or barrier semaphores. Data moves between devices by JAX's collectives and lax.ppermute only.
A program may use at most 128 MiB of HBM per device.

v0:
```python
import jax
import jax.numpy as jnp
from jax import lax
from jax.sharding import PartitionSpec as P

STEPS = 4
CAP = 8
USERS_DEV = 32


def unit_rows(matrix):
    return (matrix * lax.rsqrt(jnp.sum(matrix * matrix, axis=1, keepdims=True) + 1e-06)).astype(
        jnp.bfloat16
    )


def project_in(inputs, gate_part, up_part):

    def add_rows(piece):
        return jnp.dot(inputs, piece, preferred_element_type=jnp.float32)

    gate = add_rows(lax.all_gather(gate_part, "user", axis=0, tiled=True))
    up_proj = add_rows(lax.all_gather(up_part, "user", axis=0, tiled=True))
    return (gate, up_proj)


def shards(
    states,
    norm_gain,
    gate_weight,
    up_weight,
    down_weight,
    proj_weight,
    private_rows,
    enc_weight,
    user_ids,
):
    tok_rows, width_model = states.shape
    groups = tok_rows // STEPS
    values = states.astype(jnp.float32)
    normed = (
        values * lax.rsqrt(jnp.mean(values * values, axis=1, keepdims=True) + 1e-05) * norm_gain
    ).astype(jnp.bfloat16)
    gate_part, up_part, down_part = (gate_weight, up_weight, down_weight)
    gate, up_proj = project_in(normed, gate_part, up_part)
    hidden = (jax.nn.silu(gate) * up_proj).astype(jnp.bfloat16)
    mixed = jnp.dot(
        hidden,
        lax.all_gather(down_part, "user", axis=1, tiled=True),
        preferred_element_type=jnp.float32,
    )
    pooled_mlp = jnp.sum(mixed.reshape(-1, STEPS, width_model), axis=1)
    pooled_mlp = lax.psum_scatter(pooled_mlp, "gen", scatter_dimension=1, tiled=True)
    slab_width = pooled_mlp.shape[1]
    own_cols = lax.dynamic_slice_in_dim(values, lax.axis_index("gen") * slab_width, slab_width, 1)
    pooled_in = jnp.sum(own_cols.reshape(groups, STEPS, slab_width), axis=1)
    pooled = ((pooled_in + pooled_mlp) / STEPS).astype(jnp.bfloat16)
    partial_emb = jnp.dot(pooled, proj_weight, preferred_element_type=jnp.float32)
    embedding = lax.psum(partial_emb, "gen")
    candidate = unit_rows(embedding)
    every_cand = lax.all_gather(candidate, "user", axis=0, tiled=True)
    encoded = unit_rows(jnp.dot(private_rows, enc_weight, preferred_element_type=jnp.float32))
    scores = lax.dot_general(
        encoded, every_cand, (((1,), (1,)), ((), ())), preferred_element_type=jnp.float32
    )
    kernel = jnp.exp(scores * 60.0)
    totals = lax.psum(jnp.sum(kernel, axis=1), "cand")
    member = (user_ids[:, None] == jnp.arange(USERS_DEV, dtype=jnp.int32)[None, :]).astype(
        jnp.float32
    )
    counts = jnp.sum(member, axis=0)
    limit = jnp.minimum(1.0, CAP / jnp.maximum(counts, 1.0))
    row_cap = jnp.dot(member, limit, precision=lax.Precision.HIGHEST)
    row_total = private_rows.shape[0] * lax.axis_size("gen") * lax.axis_size("user")
    cand_total = every_cand.shape[0] * lax.axis_size("cand")
    weight_rows = row_cap / totals * (cand_total / row_total)
    partial_votes = jnp.dot(weight_rows, kernel, precision=lax.Precision.HIGHEST)
    votes = lax.psum(partial_votes, ("gen", "user"))
    return votes.reshape(lax.axis_size("user"), 1, groups)


def solution(mesh):
    return jax.shard_map(
        shards,
        mesh=mesh,
        in_specs=(
            P(("user", "cand"), None),
            P(),
            P("user", "gen"),
            P("user", "gen"),
            P("gen", "user"),
            P("gen", None),
            P(("gen", "user"), None),
            P(),
            P(("gen", "user")),
        ),
        out_specs=P(None, "cand", None),
        check_vma=False,
    )
```

profile of v0, /device:TPU:0, one launch (start us, length us, event | category | flops | bytes accessed | tf_op | source)
XLA Modules:
  0.0 810.1 jit_solution(10870717847516051505)
XLA Ops:
  6.5 0.7 all-gather.5.cloned.1.call-update
  8.8 3.1 multiply_reduce_fusion
  11.9 70.3 %all-gather.5.cloned.1.call-done = bf16[4096,896]{1,0:T(8,128)(2,1)} async-done(((bf16[256,896]{1,0:T(8,128)(2,1)}), bf16[4096,896]{1,0:T(8,128)(2,1)}) %all-gather.5.cloned.1.call-update) | async-done | bytes 7340048 | tf_op jit(solution)/shard_map/all_gather | solution.py:22
  82.2 10.1 %fusion.1 = f32[512,896]{1,0:T(8,128)} fusion(bf16[4096,896]{1,0:T(8,128)(2,1)} %all-gather.5.cloned.1.call-done, f32[4096]{0:T(1024)S(1)} %copy-done.1, f32[512]{0:T(512)S(1)} %add_rsqrt_fusion, bf16[512,4096]{1,0:T(8,128)(2,1)} %param.9), kind=kOutput, calls=%fused_computation.5 | convolution fusion | flops 3766484992 | bytes 13387776 | tf_op jit(solution)/shard_map/dot_general | solution.py:20
  92.3 63.2 %all-gather.7.cloned.1.call-done = bf16[4096,896]{1,0:T(8,128)(2,1)} async-done(((bf16[256,896]{1,0:T(8,128)(2,1)}), bf16[4096,896]{1,0:T(8,128)(2,1)}) %all-gather.7.cloned.1.call-update) | async-done | bytes 7340048 | tf_op jit(solution)/shard_map/all_gather | solution.py:23
  155.6 79.3 %all-gather.9.cloned.1.call-done = bf16[896,4096]{1,0:T(8,128)(2,1)} async-done(((bf16[896,256]{1,0:T(8,128)(2,1)}), bf16[896,4096]{1,0:T(8,128)(2,1)}) %all-gather.9.cloned.1.call-update) | async-done | bytes 7340048 | tf_op jit(solution)/shard_map/all_gather | solution.py:49
  234.8 17.4 %fusion.2 = f32[512,4096]{1,0:T(8,128)} fusion(bf16[896,4096]{1,0:T(8,128)(2,1)} %all-gather.9.cloned.1.call-done, f32[512,896]{1,0:T(8,128)} %fusion.1, bf16[4096,896]{1,0:T(8,128)(2,1)} %all-gather.7.cloned.1.call-done, f32[4096]{0:T(1024)S(1)} %copy-done.1, f32[512]{0:T(512)S(1)} %add_rsqrt_fusion, bf16[512,4096]{1,0:T(8,128)(2,1)} %param.9), kind=kOutput, calls=%fused_computation.9 | convolution fusion | flops 7527333888 | bytes 29116416 | tf_op jit(solution)/shard_map/dot_general | solution.py:47
  252.2 9.8 %reshape.32 = f32[128,4,4096]{2,1,0:T(4,128)} reshape(f32[512,4096]{1,0:T(8,128)} %fusion.2) | data formatting | bytes 16777216 | tf_op jit(solution)/shard_map/reshape | solution.py:52
  262.0 10.0 %reduce_sum.67 = f32[128,4096]{1,0:T(8,128)} reduce(f32[128,4,4096]{2,1,0:T(4,128)} %reshape.32, f32[]{:T(128)} %constant.15.clone.1), dimensions={1}, to_apply=%region_4.5 | reduce | flops 1572864 | bytes 10485764 | tf_op jit(solution)/shard_map/reduce_sum | solution.py:52
  272.1 6.5 convert_element_type.23
  278.6 1.3 constant_dynamic-slice_fusion
  279.9 1.3 reshape.31
  281.2 1.8 reduce_sum.65
  283.1 29.9 %reduce-scatter.2.cloned.1.call-done = f32[128,512]{1,0:T(8,128)} async-done(((f32[128,4096]{1,0:T(8,128)}), f32[128,512]{1,0:T(8,128)}) %reduce-scatter.2.cloned.1.call-update) | async-done | bytes 262160 | tf_op jit(solution)/shard_map/reduce_scatter | solution.py:53
  313.0 2.4 fusion.4
  315.7 70.7 %all-reduce.2.cloned.1.call-done = f32[128,1024]{1,0:T(8,128)} async-done(((f32[128,1024]{1,0:T(8,128)}), f32[128,1024]{1,0:T(8,128)}) %all-reduce.2.cloned.1.call-update) | async-done | bytes 524304 | tf_op jit(solution)/shard_map/psum | solution.py:59
  386.3 1.2 multiply_reduce_fusion.2
  387.5 1.8 multiply_convert_fusion.8
  389.5 1.8 multiply_reduce_fusion.1
  391.5 53.5 %all-gather.11.cloned.1.call-done = bf16[2048,1024]{1,0:T(8,128)(2,1)} async-done(((bf16[128,1024]{1,0:T(8,128)(2,1)}), bf16[2048,1024]{1,0:T(8,128)(2,1)}) %all-gather.11.cloned.1.call-update) | async-done | bytes 4194320 | tf_op jit(solution)/shard_map/all_gather | solution.py:61
  445.0 4.9 fusion.16
  449.8 8.8 %psum.22 = f32[256]{0:T(256)S(1)} all-reduce(f32[256]{0:T(256)S(1)} %get-tuple-element.7), channel_id=1, replica_groups=mesh['gen'=8,'user'=16,'cand'=2] {'cand'}, use_global_device_ids=true, to_apply=%region_9.10 | all-reduce | flops 256 | bytes 2048 | tf_op jit(solution)/shard_map/psum | solution.py:67
  458.6 2.7 convolution_bitcast_fusion
  461.3 341.9 %psum.23 = f32[16,1,128]{2,1,0:T(1,128)} all-reduce(f32[16,1,128]{2,1,0:T(1,128)S(1)} %convolution_bitcast_fusion), channel_id=1, replica_groups=mesh['gen'=8,'user'=16,'cand'=2] {'gen','user'}, use_global_device_ids=true, to_apply=%region_10.11 | all-reduce | flops 2048 | bytes 16384 | tf_op jit(solution)/shard_map/psum | solution.py:78
  (23 shorter events, 2.1 us)
Async XLA Ops:
  6.5 383.0 %copy-start = (bf16[1024,1024]{1,0:T(8,128)(2,1)S(1)}, bf16[1024,1024]{1,0:T(8,128)(2,1)}, u32[]{:S(2)}) copy-start(bf16[1024,1024]{1,0:T(8,128)(2,1)} %param.16) | copy-start | bytes 6291460
  6.5 75.7 %copy-start.1 = (f32[4096]{0:T(1024)S(1)}, f32[4096]{0:T(1024)}, u32[]{:S(2)}) copy-start(f32[4096]{0:T(1024)} %param.10) | copy-start | bytes 49156
  6.5 75.7 %all-gather.5.cloned.1.call-start = ((), (), s32[]{:S(2)}) async-start(), calls=%async_computation.1 | async-start | bytes 7798784 | tf_op jit(solution)/shard_map/all_gather | solution.py:22
  7.3 148.3 %all-gather.7.cloned.1.call-start = ((), (), s32[]{:S(2)}) async-start(), calls=%async_computation.2 | async-start | bytes 7798784 | tf_op jit(solution)/shard_map/all_gather | solution.py:23
  8.0 226.8 %all-gather.9.cloned.1.call-start = ((), (), s32[]{:S(2)}) async-start(), calls=%async_computation.3 | async-start | bytes 7798784 | tf_op jit(solution)/shard_map/all_gather | solution.py:49
  8.7 304.2 %reduce-scatter.2.cloned.1.call-start = ((), (), s32[]{:S(2)}) async-start(), calls=%async_computation.4 | async-start | bytes 2359296 | tf_op jit(solution)/shard_map/reduce_scatter | solution.py:53
  272.1 114.3 %all-reduce.2.cloned.1.call-start = ((), (), s32[]{:S(2)}) async-start(), calls=%async_computation.5 | async-start | bytes 1048576 | tf_op jit(solution)/shard_map/psum | solution.py:59
  279.9 109.5 %copy-start.2 = (s32[256]{0:T(256)S(1)}, s32[256]{0:T(256)}, u32[]{:S(2)}) copy-start(s32[256]{0:T(256)} %param.17) | copy-start | bytes 3076
  315.4 129.5 %all-gather.11.cloned.1.call-start = ((), (), s32[]{:S(2)}) async-start(), calls=%async_computation.6 | async-start | bytes 4456448 | tf_op jit(solution)/shard_map/all_gather | solution.py:61
Sparse Core Ops, SparseCore 0:
  9.8 72.3 all-gather.4
  84.7 70.8 all-gather.6
  158.0 76.7 all-gather.8
  272.2 40.7 reduce-scatter.1
  315.5 70.7 all-reduce.1
  389.5 55.4 all-gather.10
where the time goes:
time: 811 us; the launch traced here: 810 us
  waiting for transfers between devices  369 us (45%)
  blocking collectives  351 us (43%)
  matrix products  39.5 us (5%)
  other arithmetic  24.6 us (3%)
  between operations  13.5 us (2%)
  local copies, waits for them, and re-layouts  12.4 us (2%)
    psum x1, blocking collectives, shards(): votes = lax.psum(partial_votes, ('gen', 'user'))  342 us
    all_gather x1, waiting for transfers between devices, shards(): lax.all_gather(down_part, 'user', axis=1, tiled=True)  79.3 us
    psum x1, waiting for transfers between devices, shards(): embedding = lax.psum(partial_emb, 'gen')  70.7 us
    all_gather x1, waiting for transfers between devices, project_in(): gate = add_rows(lax.all_gather(gate_part, 'user', axis=0, tiled=True))  70.3 us
    all_gather x1, waiting for transfers between devices, project_in(): up_proj = add_rows(lax.all_gather(up_part, 'user', axis=0, tiled=True))  63.2 us
    all_gather x1, waiting for transfers between devices, shards(): every_cand = lax.all_gather(candidate, 'user', axis=0, tiled=True)  53.5 us
    reduce_scatter x1, waiting for transfers between devices, shards(): lax.psum_scatter(pooled_mlp, 'gen', scatter_dimension=1, tiled=True)  29.9 us
    dot_general x1, matrix products, shards(): jnp.dot(hidden, lax.all_gather(down_part, 'user', axis=1, tiled=True), pr...  17.4 us
  transfers between devices with their start and end apart: 6, of which 6 were waited for; matrix products, arithmetic and copies ran while one was open for 3% of the time, Pallas kernels for 0%

commit v1 on v0

--- a/solution.py
+++ b/solution.py
@@ -6,6 +6,12 @@
 STEPS = 4
 CAP = 8
 USERS_DEV = 32
+
+
+def gathered_along(block, name, d):
+    parts = lax.all_gather(block, name, axis=0, tiled=False)
+    full = jnp.concatenate(parts, axis=d)
+    return full
 
 
 def unit_rows(matrix):
@@ -45,9 +51,7 @@
     gate, up_proj = project_in(normed, gate_part, up_part)
     hidden = (jax.nn.silu(gate) * up_proj).astype(jnp.bfloat16)
     mixed = jnp.dot(
-        hidden,
-        lax.all_gather(down_part, "user", axis=1, tiled=True),
-        preferred_element_type=jnp.float32,
+        hidden, gathered_along(down_part, "user", 1), preferred_element_type=jnp.float32
     )
     pooled_mlp = jnp.sum(mixed.reshape(-1, STEPS, width_model), axis=1)
     pooled_mlp = lax.psum_scatter(pooled_mlp, "gen", scatter_dimension=1, tiled=True)

time: 811 us -> 789 us (0.973)
  waiting for transfers between devices: 369 us -> 351 us
  other arithmetic: 24.6 us -> 14.6 us
    all_gather x1, waiting for transfers between devices: 79.3 us -> 61.3 us  [gathered_along(): parts = lax.all_gather(block, name, axis=0, tiled=False)]
    dot_general x1 -> x2, matrix products: 10.1 us -> 20.4 us  [add_rows(): return jnp.dot(inputs, piece, preferred_element_type=jnp.float32)]
    reduce_sum x1 -> x0, other arithmetic: 10 us -> none  [shards(): pooled_mlp = jnp.sum(mixed.reshape(-1, STEPS, width_model), axis=1)]
  transfers between devices with their start and end apart: 6 -> 6, of which waited for: 6 -> 6; matrix products, arithmetic and copies ran while one was open for 3% -> 5% of each run, Pallas kernels for 0% -> 0%
where the time goes in v1:
time: 789 us; the launch traced here: 788 us
  waiting for transfers between devices  351 us (44%)
  blocking collectives  351 us (44%)
  matrix products  41.7 us (5%)
  local copies, waits for them, and re-layouts  15.5 us (2%)
  other arithmetic  14.6 us (2%)
  between operations  13.5 us (2%)
    psum x1, blocking collectives, shards(): votes = lax.psum(partial_votes, ('gen', 'user'))  342 us
    psum x1, waiting for transfers between devices, shards(): embedding = lax.psum(partial_emb, 'gen')  71.1 us
    all_gather x1, waiting for transfers between devices, project_in(): gate = add_rows(lax.all_gather(gate_part, 'user', axis=0, tiled=True))  70.3 us
    all_gather x1, waiting for transfers between devices, project_in(): up_proj = add_rows(lax.all_gather(up_part, 'user', axis=0, tiled=True))  63.2 us
    all_gather x1, waiting for transfers between devices, gathered_along(): parts = lax.all_gather(block, name, axis=0, tiled=False)  61.3 us
    all_gather x1, waiting for transfers between devices, shards(): every_cand = lax.all_gather(candidate, 'user', axis=0, tiled=True)  53.5 us
    reduce_scatter x1, waiting for transfers between devices, shards(): lax.psum_scatter(pooled_mlp, 'gen', scatter_dimension=1, tiled=True)  30 us
    dot_general x2, matrix products, add_rows(): return jnp.dot(inputs, piece, preferred_element_type=jnp.float32)  20.4 us
  transfers between devices with their start and end apart: 6, of which 6 were waited for; matrix products, arithmetic and copies ran while one was open for 5% of the time, Pallas kernels for 0%

profile of v1, /device:TPU:0, one launch (start us, length us, event | category | flops | bytes accessed | tf_op | source)
XLA Modules:
  0.0 787.9 jit_solution(11399392616675531968)
XLA Ops:
  8.8 3.1 multiply_reduce_fusion
  11.9 70.3 %all-gather.6.cloned.1.call-done = bf16[4096,896]{1,0:T(8,128)(2,1)} async-done(((bf16[256,896]{1,0:T(8,128)(2,1)}), bf16[4096,896]{1,0:T(8,128)(2,1)}) %all-gather.6.cloned.1.call-update) | async-done | bytes 7340048 | tf_op jit(solution)/shard_map/all_gather | solution.py:28
  82.2 10.2 %fusion.1 = f32[512,896]{1,0:T(8,128)} fusion(bf16[4096,896]{1,0:T(8,128)(2,1)} %all-gather.6.cloned.1.call-done, f32[4096]{0:T(1024)S(1)} %copy-done.1, f32[512]{0:T(512)S(1)} %add_rsqrt_fusion, bf16[512,4096]{1,0:T(8,128)(2,1)} %param.9), kind=kOutput, calls=%fused_computation.6 | convolution fusion | flops 3766484992 | bytes 13387776 | tf_op jit(solution)/shard_map/dot_general | solution.py:26
  92.4 63.2 %all-gather.8.cloned.1.call-done = bf16[4096,896]{1,0:T(8,128)(2,1)} async-done(((bf16[256,896]{1,0:T(8,128)(2,1)}), bf16[4096,896]{1,0:T(8,128)(2,1)}) %all-gather.8.cloned.1.call-update) | async-done | bytes 7340048 | tf_op jit(solution)/shard_map/all_gather | solution.py:29
  155.6 10.3 %multiply_convert_fusion.1 = bf16[512,896]{1,0:T(8,128)(2,1)} fusion(f32[512,896]{1,0:T(8,128)} %fusion.1, bf16[4096,896]{1,0:T(8,128)(2,1)} %all-gather.8.cloned.1.call-done, f32[4096]{0:T(1024)S(1)} %copy-done.1, f32[512]{0:T(512)S(1)} %add_rsqrt_fusion, bf16[512,4096]{1,0:T(8,128)(2,1)} %param.9), kind=kOutput, calls=%fused_computation.5 | convolution fusion | flops 3769237504 | bytes 14305280 | tf_op jit(solution)/shard_map/dot_general | solution.py:26
  165.8 1.8 dot_general.30
  167.6 61.3 %all-gather.12.cloned.1.call-done = bf16[14336,256]{1,0:T(8,128)(2,1)} async-done(((bf16[896,256]{1,0:T(8,128)(2,1)}), bf16[14336,256]{1,0:T(8,128)(2,1)}) %all-gather.12.cloned.1.call-update) | async-done | bytes 7340048 | tf_op jit(solution)/shard_map/all_gather | solution.py:12
  228.9 11.1 %copy.13 = bf16[896,16,256]{0,2,1:T(8,128)(2,1)} copy(bf16[896,16,256]{2,0,1:T(8,128)(2,1)} %bitcast.24) | data formatting | bytes 14680064 | tf_op jit(solution)/shard_map/reshape | solution.py:13
  240.1 9.3 %convolution_reduce_fusion = f32[128,4096]{1,0:T(8,128)} fusion(bf16[896,4096,1]{0,1,2:T(8,128)(2,1)} %bitcast.25, bf16[128,4,896]{2,1,0:T(4,128)(2,1)S(1)} %dot_general.30), kind=kOutput, calls=%fused_computation.4 | convolution fusion | flops 3759669248 | bytes 10354688 | tf_op jit(solution)/shard_map/dot_general | solution.py:53
  249.6 6.5 convert_element_type.23
  256.1 1.3 constant_dynamic-slice_fusion
  257.4 1.3 reshape.36
  258.7 1.8 reduce_sum.65
  260.6 30.0 %reduce-scatter.2.cloned.1.call-done = f32[128,512]{1,0:T(8,128)} async-done(((f32[128,4096]{1,0:T(8,128)}), f32[128,512]{1,0:T(8,128)}) %reduce-scatter.2.cloned.1.call-update) | async-done | bytes 262160 | tf_op jit(solution)/shard_map/reduce_scatter | solution.py:57
  290.6 2.4 fusion.4
  293.1 71.1 %all-reduce.2.cloned.1.call-done = f32[128,1024]{1,0:T(8,128)} async-done(((f32[128,1024]{1,0:T(8,128)}), f32[128,1024]{1,0:T(8,128)}) %all-reduce.2.cloned.1.call-update) | async-done | bytes 524304 | tf_op jit(solution)/shard_map/psum | solution.py:63
  364.2 1.2 multiply_reduce_fusion.2
  365.3 1.8 multiply_convert_fusion.6
  367.3 1.8 multiply_reduce_fusion.1
  369.3 53.5 %all-gather.10.cloned.1.call-done = bf16[2048,1024]{1,0:T(8,128)(2,1)} async-done(((bf16[128,1024]{1,0:T(8,128)(2,1)}), bf16[2048,1024]{1,0:T(8,128)(2,1)}) %all-gather.10.cloned.1.call-update) | async-done | bytes 4194320 | tf_op jit(solution)/shard_map/all_gather | solution.py:65
  422.8 4.9 fusion.15
  427.6 8.8 %psum.22 = f32[256]{0:T(256)S(1)} all-reduce(f32[256]{0:T(256)S(1)} %get-tuple-element.7), channel_id=1, replica_groups=mesh['gen'=8,'user'=16,'cand'=2] {'cand'}, use_global_device_ids=true, to_apply=%region_9.10 | all-reduce | flops 256 | bytes 2048 | tf_op jit(solution)/shard_map/psum | solution.py:71
  436.5 2.7 convolution_bitcast_fusion
  439.1 341.9 %psum.23 = f32[16,1,128]{2,1,0:T(1,128)} all-reduce(f32[16,1,128]{2,1,0:T(1,128)S(1)} %convolution_bitcast_fusion), channel_id=1, replica_groups=mesh['gen'=8,'user'=16,'cand'=2] {'gen','user'}, use_global_device_ids=true, to_apply=%region_10.11 | all-reduce | flops 2048 | bytes 16384 | tf_op jit(solution)/shard_map/psum | solution.py:82
  (24 shorter events, 2.8 us)
Async XLA Ops:
  6.5 360.8 %copy-start = (bf16[1024,1024]{1,0:T(8,128)(2,1)S(1)}, bf16[1024,1024]{1,0:T(8,128)(2,1)}, u32[]{:S(2)}) copy-start(bf16[1024,1024]{1,0:T(8,128)(2,1)} %param.16) | copy-start | bytes 6291460
  6.5 75.7 %copy-start.1 = (f32[4096]{0:T(1024)S(1)}, f32[4096]{0:T(1024)}, u32[]{:S(2)}) copy-start(f32[4096]{0:T(1024)} %param.10) | copy-start | bytes 49156
  6.5 75.7 %all-gather.6.cloned.1.call-start = ((), (), s32[]{:S(2)}) async-start(), calls=%async_computation.1 | async-start | bytes 7798784 | tf_op jit(solution)/shard_map/all_gather | solution.py:28
  7.3 148.3 %all-gather.8.cloned.1.call-start = ((), (), s32[]{:S(2)}) async-start(), calls=%async_computation.2 | async-start | bytes 7798784 | tf_op jit(solution)/shard_map/all_gather | solution.py:29
  8.0 220.9 %all-gather.12.cloned.1.call-start = ((), (), s32[]{:S(2)}) async-start(), calls=%async_computation.6 | async-start | bytes 7798784 | tf_op jit(solution)/shard_map/all_gather | solution.py:12
  8.7 281.8 %reduce-scatter.2.cloned.1.call-start = ((), (), s32[]{:S(2)}) async-start(), calls=%async_computation.3 | async-start | bytes 2359296 | tf_op jit(solution)/shard_map/reduce_scatter | solution.py:57
  249.4 114.8 %all-reduce.2.cloned.1.call-start = ((), (), s32[]{:S(2)}) async-start(), calls=%async_computation.4 | async-start | bytes 1048576 | tf_op jit(solution)/shard_map/psum | solution.py:63
  257.4 109.8 %copy-start.2 = (s32[256]{0:T(256)S(1)}, s32[256]{0:T(256)}, u32[]{:S(2)}) copy-start(s32[256]{0:T(256)} %param.17) | copy-start | bytes 3076
  293.0 129.7 %all-gather.10.cloned.1.call-start = ((), (), s32[]{:S(2)}) async-start(), calls=%async_computation.5 | async-start | bytes 4456448 | tf_op jit(solution)/shard_map/all_gather | solution.py:65
Sparse Core Ops, SparseCore 0:
  9.8 72.3 all-gather.5
  84.7 70.8 all-gather.7
  158.1 70.8 all-gather.11
  249.5 41.0 reduce-scatter.1
  293.2 70.9 all-reduce.1
  367.3 55.4 all-gather.9
